TPU v7x, 256 devices: a whole 4x4x8 slice. The times are simulated.
256 devices in a mesh: row: 16 (over x_lo, z), col: 16 (over x_hi, y, core).
Axes of the slice: x: 4 (x_hi: 2, x_lo: 2; x = x_hi * 2 + x_lo), y: 4, z: 8, core: 2. Of those that a mesh axis runs over, the one named last changes fastest.
Arguments:
- adjoints: bfloat16 [4096, 16, 200], P(('row', 'col')), may hold values from -6 to 6
- jac_blocks: bfloat16 [16, 16, 128, 200, 200], P('row', 'col'), may hold values from -0.4375 to 0.4375
- jac_rows: int32 [16, 16, 128], P('row', 'col'), may hold values from 0 to 255, as said below
- jac_cols: int32 [16, 16, 128], P('row', 'col'), may hold values from 0 to 255, as said below
- tile_count: int32 [16, 16], P('row', 'col'), may hold values from 32 to 128, as said below
Outputs:
- transposed: bfloat16 [4096, 16, 200], P('col')
Inputs may be any that keep to these rules, and one draw needn't show every extreme that they name: `jac_rows`: row faces within a tile; both ends are named by some slot. `jac_cols`: column faces within a tile; both ends are named by some slot. `tile_count`: slots at or above the count are padding and are ignored; some tile has exactly 128 live slots.
All inputs are finite; a program needn't handle non-finite values.
Results may differ from a plain program's by a relative error of at most 0.001.
Values may be sent and summed in bfloat16 or wider, within the bound.
No kernel may reach another device: no remote copies, remote signals or barrier semaphores. Data moves between devices by JAX's collectives and lax.ppermute only.
A program may use at most 64 MiB of HBM per device.

v0:
```python
import jax
import jax.numpy as jnp
from jax import lax
from jax.sharding import PartitionSpec as P


def add_columns(selector, products):
    return jnp.einsum(
        "cs,ske->cke",
        selector,
        products,
        preferred_element_type=jnp.float32,
        precision=lax.Precision.HIGHEST,
    )


def on_device(adjoints, jac_blocks, jac_rows, jac_cols, tile_count):
    row_block = lax.all_gather(adjoints, "col", axis=0, tiled=True)
    blocks = jac_blocks[0, 0]
    slot_rows = jac_rows[0, 0]
    slot_cols = jac_cols[0, 0]
    live_count = tile_count[0, 0]
    slot_count = slot_rows.shape[0]
    faces_here = adjoints.shape[0]
    column_count = faces_here * lax.axis_size("row")
    picked = jnp.take(row_block, slot_rows, axis=0)
    products = jnp.einsum("skd,sde->ske", picked, blocks, preferred_element_type=jnp.float32)
    live_slot = jnp.arange(slot_count, dtype=jnp.int32) < live_count
    matches = live_slot[None, :] & (
        slot_cols[None, :] == jnp.arange(column_count, dtype=jnp.int32)[:, None]
    )
    partial_value = add_columns(matches.astype(jnp.float32), products)
    summed = lax.psum(partial_value, "row")
    return summed.astype(jnp.bfloat16)


def solution(mesh):
    placed = (
        P(("row", "col"), None, None),
        P("row", "col", None, None, None),
        P("row", "col", None),
        P("row", "col", None),
        P("row", "col"),
    )
    return jax.shard_map(
        on_device, mesh=mesh, in_specs=placed, out_specs=P("col", None, None), check_vma=False
    )
```

profile of v0, /device:TPU:2, one launch (start us, length us, event | category | flops | bytes accessed | tf_op | source)
XLA Modules:
  0.0 172.7 jit_solution(8518587678829528338)
XLA Ops:
  6.5 0.0 all-gather.2.cloned.1.call-start
  6.5 0.7 all-gather.2.cloned.1.call-update
  7.9 0.0 copy-start.1
  7.9 19.1 %copy.6 = bf16[128,200,200]{2,1,0:T(8,128)(2,1)} copy(bf16[128,200,200]{0,2,1:T(8,128)(2,1)} %bitcast.15) | data formatting | bytes 20480000 | tf_op jit(solution)/shard_map/squeeze | solution.py:19
  27.0 0.0 copy-done.1
  27.1 37.7 %all-gather.2.cloned.1.call-done = bf16[256,16,200]{2,1,0:T(8,128)(2,1)} async-done(((bf16[16,16,200]{2,1,0:T(8,128)(2,1)}), bf16[256,16,200]{2,1,0:T(8,128)(2,1)}) %all-gather.2.cloned.1.call-update) | async-done | bytes 1638416 | tf_op jit(solution)/shard_map/all_gather | solution.py:18
  64.7 2.2 %gather_fusion = bf16[128,16,200]{2,1,0:T(8,128)(2,1)S(1)} fusion(bf16[256,16,200]{2,1,0:T(8,128)(2,1)} %all-gather.2.cloned.1.call-done, s32[1024]{0:T(1024)S(1)} %pad_clamp_fusion), kind=kCustom, calls=%fused_computation | custom fusion | bytes 1638912 | tf_op jit(solution)/shard_map/jit(_take)/gather | solution.py:26
  67.0 6.7 %fusion = f32[128,16,200]{2,1,0:T(8,128)S(1)} fusion(bf16[128,200,200]{2,1,0:T(8,128)(2,1)} %copy.6, bf16[128,16,200]{2,1,0:T(8,128)(2,1)S(1)} %gather_fusion, pred[128]{0:T(512)(128)(4,1)S(1)} %compare_and_fusion), kind=kOutput, calls=%fused_computation.1 | convolution fusion | flops 164249600 | bytes 12697728 | tf_op jit(solution)/shard_map/skd,sde->ske/dot_general | solution.py:27
  73.7 0.0 copy-start
  73.7 1.8 %copy.7 = f32[128,16,200]{0,2,1:T(8,128)} copy(f32[128,16,200]{2,1,0:T(8,128)S(1)} %fusion) | data formatting | bytes 3276800 | tf_op jit(solution)/shard_map/skd,sde->ske/dot_general | solution.py:27
  75.5 0.0 copy-done
  75.5 2.9 %fusion.5 = f32[256,3200]{0,1:S(1)} fusion(f32[128,3200]{0,1:T(8,128)} %bitcast.16, s32[128]{0:T(128)S(1)} %bitcast.17, pred[128]{0:T(512)(128)(4,1)S(1)} %iota_compare_fusion.1), kind=kOutput, calls=%fused_computation.7 | convolution fusion | flops 1258356736 | bytes 4915840
  78.4 87.5 %all-reduce.1 = bf16[256,16,200]{0,2,1:T(8,128)(2,1)} all-reduce(f32[256,16,200]{0,2,1:T(8,128)S(1)} %bitcast.14), channel_id=1, replica_groups=mesh['row'=16,'col'=16] {'row'}, use_global_device_ids=true, to_apply=%region_0.1 | all-reduce | flops 819200 | bytes 4915200 | tf_op jit(solution)/shard_map/psum | solution.py:33
  (4 shorter events, 0.0 us)
Async XLA Ops:
  6.5 58.2 %all-gather.2.cloned.1.call-start = ((), (), s32[]{:S(2)}) async-start(), calls=%async_computation | async-start | bytes 2228224 | tf_op jit(solution)/shard_map/all_gather | solution.py:18
  7.9 19.1 %copy-start.1 = (s32[1,1,128]{2,1,0:T(1,128)S(1)}, s32[1,1,128]{2,1,0:T(1,128)}, u32[]{:S(2)}) copy-start(s32[1,1,128]{2,1,0:T(1,128)} %param.7) | copy-start | bytes 1540
  73.7 1.8 %copy-start = (s32[1,1,128]{2,1,0:T(1,128)S(1)}, s32[1,1,128]{2,1,0:T(1,128)}, u32[]{:S(2)}) copy-start(s32[1,1,128]{2,1,0:T(1,128)} %param.8) | copy-start | bytes 1540
Sparse Core Ops, SparseCore 0:
  10.1 54.6 all-gather.1
where the time goes:
time: 173 us
  blocking collectives  87.5 us (51%)
  waiting for transfers between devices  38.4 us (22%)
  local copies, waits for them, and re-layouts  23.1 us (13%)
  between operations  14.1 us (8%)
  matrix products  9.58 us (6%)
    psum x1, blocking collectives, on_device(): summed = lax.psum(partial_value, 'row')  87.5 us
    all_gather x1, waiting for transfers between devices, on_device(): row_block = lax.all_gather(adjoints, 'col', axis=0, tiled=True)  37.7 us
    squeeze x1, local copies, waits for them, and re-layouts, on_device(): blocks = jac_blocks[0, 0]  19.1 us
    dot_general x1, matrix products, on_device(): jnp.einsum('skd,sde->ske', picked, blocks, preferred_element_type=jnp.flo...  6.7 us
  transfers between devices with their start and end apart: 1, of which 1 were waited for; matrix products, arithmetic and copies ran while one was open for 11% of the time, Pallas kernels for 0%

commit v1 on v0

--- a/solution.py
+++ b/solution.py
@@ -15,7 +15,9 @@
 
 
 def on_device(adjoints, jac_blocks, jac_rows, jac_cols, tile_count):
-    row_block = lax.all_gather(adjoints, "col", axis=0, tiled=True)
+    row_block = jnp.concatenate(
+        lax.all_to_all(jnp.stack([adjoints] * lax.axis_size("col")), "col", 0, 0), axis=0
+    )
     blocks = jac_blocks[0, 0]
     slot_rows = jac_rows[0, 0]
     slot_cols = jac_cols[0, 0]

time: 173 us -> 141 us (0.82)
  waiting for transfers between devices: 38.4 us -> 9.94 us
  between operations: 14.1 us -> 0.71 us
  starting transfers between devices: 0.01 us -> 6.14 us
    all_gather x1 -> x0, waiting for transfers between devices: 37.7 us -> none  [on_device(): row_block = lax.all_gather(adjoints, 'col', axis=0, tiled=True)]
    all_to_all x0 -> x1, waiting for transfers between devices: none -> 9.94 us  [on_device(): lax.all_to_all(jnp.stack([adjoints] * lax.axis_size('col')), 'col', 0, 0)]
    all_to_all x0 -> x1, starting transfers between devices: none -> 6.14 us  [on_device(): lax.all_to_all(jnp.stack([adjoints] * lax.axis_size('col')), 'col', 0, 0)]
    another operation x0 -> x1, local copies, waits for them, and re-layouts: none -> 2.42 us  [on_device(): jnp.stack([adjoints] * lax.axis_size('col'))]
  transfers between devices with their start and end apart: 1 -> 1, of which waited for: 1 -> 1; matrix products, arithmetic and copies ran while one was open for 11% -> 14% of each run, Pallas kernels for 0% -> 0%
where the time goes in v1:
time: 141 us; the launch traced here: 139 us
  blocking collectives  88.9 us (63%)
  local copies, waits for them, and re-layouts  24 us (17%)
  waiting for transfers between devices  9.94 us (7%)
  matrix products  9.58 us (7%)
  starting transfers between devices  6.14 us (4%)
    psum x1, blocking collectives, on_device(): summed = lax.psum(partial_value, 'row')  88.9 us
    squeeze x1, local copies, waits for them, and re-layouts, on_device(): blocks = jac_blocks[0, 0]  19.1 us
    all_to_all x1, waiting for transfers between devices, on_device(): lax.all_to_all(jnp.stack([adjoints] * lax.axis_size('col')), 'col', 0, 0)  9.94 us
    dot_general x1, matrix products, on_device(): jnp.einsum('skd,sde->ske', picked, blocks, preferred_element_type=jnp.flo...  6.7 us
    all_to_all x1, starting transfers between devices, on_device(): lax.all_to_all(jnp.stack([adjoints] * lax.axis_size('col')), 'col', 0, 0)  6.14 us
    unnamed x1, matrix products  2.89 us
  transfers between devices with their start and end apart: 1, of which 1 were waited for; matrix products, arithmetic and copies ran while one was open for 14% of the time, Pallas kernels for 0%

profile of v1, /device:TPU:2, one launch (start us, length us, event | category | flops | bytes accessed | tf_op | source)
XLA Modules:
  0.0 139.3 jit_solution(16399536258181379346)
XLA Ops:
  0.0 2.4 %stack.2 = bf16[16,16,16,200]{3,2,1,0:T(8,128)(2,1)} broadcast(bf16[16,16,200]{2,1,0:T(8,128)(2,1)} %param.5), dimensions={1,2,3} | broadcast | bytes 1740800 | tf_op jit(solution)/shard_map/stack | solution.py:19
  2.4 6.1 %all-to-all-start = ((bf16[16,16,16,200]{3,2,1,0:T(8,128)(2,1)}), bf16[16,16,16,200]{3,2,1,0:T(8,128)(2,1)S(1)}, u32[]{:S(2)}, u32[]{:S(2)}) async-start(bf16[16,16,16,200]{3,2,1,0:T(8,128)(2,1)} %stack.2), calls=%async_computation | async-start | bytes 4194304 | tf_op jit(solution)/shard_map/all_to_all | solution.py:19
  9.2 0.0 copy-start.1
  9.2 19.1 %copy.6 = bf16[128,200,200]{2,1,0:T(8,128)(2,1)} copy(bf16[128,200,200]{0,2,1:T(8,128)(2,1)} %bitcast.16) | data formatting | bytes 20480000 | tf_op jit(solution)/shard_map/squeeze | solution.py:21
  28.3 0.0 copy-done.1
  28.4 9.9 %all-to-all-done = bf16[16,16,16,200]{3,2,1,0:T(8,128)(2,1)S(1)} async-done(((bf16[16,16,16,200]{3,2,1,0:T(8,128)(2,1)}), bf16[16,16,16,200]{3,2,1,0:T(8,128)(2,1)S(1)}, u32[]{:S(2)}, u32[]{:S(2)}) %all-to-all-start) | async-done | bytes 1638432 | tf_op jit(solution)/shard_map/all_to_all | solution.py:19
  38.3 0.6 gather_fusion
  39.0 6.7 %fusion = f32[128,16,200]{2,1,0:T(8,128)S(1)} fusion(bf16[128,200,200]{2,1,0:T(8,128)(2,1)} %copy.6, bf16[128,16,200]{2,1,0:T(8,128)(2,1)S(1)} %gather_fusion, pred[128]{0:T(512)(128)(4,1)S(1)} %compare_and_fusion), kind=kOutput, calls=%fused_computation.1 | convolution fusion | flops 164249600 | bytes 12697728 | tf_op jit(solution)/shard_map/skd,sde->ske/dot_general | solution.py:29
  45.7 0.0 copy-start
  45.7 1.8 %copy.7 = f32[128,16,200]{0,2,1:T(8,128)} copy(f32[128,16,200]{2,1,0:T(8,128)S(1)} %fusion) | data formatting | bytes 3276800 | tf_op jit(solution)/shard_map/skd,sde->ske/dot_general | solution.py:29
  47.5 0.0 copy-done
  47.5 2.9 %fusion.5 = f32[256,3200]{0,1:S(1)} fusion(f32[128,3200]{0,1:T(8,128)} %bitcast.17, s32[128]{0:T(128)S(1)} %bitcast.19, pred[128]{0:T(512)(128)(4,1)S(1)} %iota_compare_fusion.1), kind=kOutput, calls=%fused_computation.7 | convolution fusion | flops 1258356736 | bytes 4915840
  50.4 88.9 %all-reduce.1 = bf16[256,16,200]{0,2,1:T(8,128)(2,1)} all-reduce(f32[256,16,200]{0,2,1:T(8,128)S(1)} %bitcast.15), channel_id=1, replica_groups=mesh['row'=16,'col'=16] {'row'}, use_global_device_ids=true, to_apply=%region_0.1 | all-reduce | flops 819200 | bytes 4915200 | tf_op jit(solution)/shard_map/psum | solution.py:35
  (4 shorter events, 0.0 us)
Async XLA Ops:
  2.4 35.9 %all-to-all-start = ((bf16[16,16,16,200]{3,2,1,0:T(8,128)(2,1)}), bf16[16,16,16,200]{3,2,1,0:T(8,128)(2,1)S(1)}, u32[]{:S(2)}, u32[]{:S(2)}) async-start(bf16[16,16,16,200]{3,2,1,0:T(8,128)(2,1)} %stack.2), calls=%async_computation | async-start | bytes 4194304 | tf_op jit(solution)/shard_map/all_to_all | solution.py:19
  9.2 19.1 %copy-start.1 = (s32[1,1,128]{2,1,0:T(1,128)S(1)}, s32[1,1,128]{2,1,0:T(1,128)}, u32[]{:S(2)}) copy-start(s32[1,1,128]{2,1,0:T(1,128)} %param.7) | copy-start | bytes 1540
  45.7 1.8 %copy-start = (s32[1,1,128]{2,1,0:T(1,128)S(1)}, s32[1,1,128]{2,1,0:T(1,128)}, u32[]{:S(2)}) copy-start(s32[1,1,128]{2,1,0:T(1,128)} %param.8) | copy-start | bytes 1540
